TPU v7x, 32 devices: a whole 2x2x4 slice. The times are simulated.
32 devices in a mesh: gx: 4 (over z), gy: 4 (over x, core), gz: 2 (over y).
Axes of the slice: x: 2, y: 2, z: 4, core: 2. Of those that a mesh axis runs over, the one named last changes fastest.
Arguments:
- element_ops: float32 [64, 64, 4096], P(None, None, ('gx', 'gy', 'gz')), may hold values from -0.5 to 48, as said below
- load_terms: float32 [64, 4096], P(None, ('gx', 'gy', 'gz')), may hold values from -16 to 16
- trial_velocity: float32 [3, 512, 4096], P(None, None, ('gx', 'gy', 'gz')), may hold values from -16 to 16
- tracer_coords: float32 [3, 65536], P(None, ('gx', 'gy', 'gz')), may hold values from -1 to 1
- tracer_old_velocity: float32 [3, 65536], P(None, ('gx', 'gy', 'gz')), may hold values from -6 to 6
- host_line: int32 [65536, 1], P(('gx', 'gy', 'gz')), may hold values from 0 to 3; in each aligned block of 2048 rows (0 to 2047, 2048 to 4095, ...) at most 1024 rows name the same one
- host_element_index: int32 [65536], P(('gx', 'gy', 'gz')), may hold values from 0 to 127
Outputs:
- pressure_fix: float32 [64, 4096], P(None, ('gx', 'gy', 'gz'))
- velocity: bfloat16 [3, 512, 4096], P(None, None, ('gx', 'gy', 'gz'))
- residual_power: float32 [], replicated
- tracer_velocity: float32 [3, 65536], P(None, ('gx', 'gy', 'gz'))
- new_coords: float32 [3, 65536], P(None, ('gx', 'gy', 'gz'))
Inputs may be any that keep to these rules, and one draw needn't show every extreme that they name: `element_ops`: symmetric in its first two dimensions; every diagonal entry exceeds the sum of the magnitudes of the other entries of its row. `host_line`: among the 2048 tracers of one device, no host position is named more than 1024 times, a bound that some block reaches in every draw.
All inputs are finite; a program needn't handle non-finite values. Where the computation divides by a largest or mean magnitude, that divisor is 1e-20 or more.
Results may differ from a plain program's by a relative error of at most 0.0029.
Values may be sent and summed in bfloat16 or wider, within the bound.
A program may use at most 64 MiB of HBM per device.

v0:
```python
import functools

import jax
import jax.numpy as jnp
import numpy as np
from jax import lax
from jax.experimental import pallas as pl
from jax.experimental.pallas import tpu as pltpu
from jax.sharding import PartitionSpec as P

EX = 4
EY = 4
EZ = 8
SWEEPS = 4
NODES = 64
FACE = 16
LANES = 128
FINE = 512

lower_bound = 0.25
upper_bound = 2.0
courant = 0.5
AXES = ("gx", "gy", "gz")
COUNTS = (EX, EY, EZ)
STEPS = (EY * EZ, EZ, 1)
MESH = pl.DeviceIdType.MESH


def node_tables():
    coarse = -np.cos(np.pi * np.arange(4) / 3.0)
    fine = -np.cos(np.pi * np.arange(8) / 7.0)
    plain = np.zeros((8, 4))
    slope = np.zeros((8, 4))
    for target in range(8):
        for source in range(4):
            others = [other for other in range(4) if other != source]
            value = 1.0
            for other in others:
                value *= (fine[target] - coarse[other]) / (coarse[source] - coarse[other])
            plain[target, source] = value
            total = 0.0
            for skipped in others:
                term = 1.0 / (coarse[source] - coarse[skipped])
                for other in others:
                    if other != skipped:
                        term *= (fine[target] - coarse[other]) / (coarse[source] - coarse[other])
                total += term
            slope[target, source] = total
    return plain, slope, fine


def gradient_matrix():
    plain, slope, _ = node_tables()
    rows = [
        np.kron(np.kron(slope, plain), plain),
        np.kron(np.kron(plain, slope), plain),
        np.kron(np.kron(plain, plain), slope),
    ]
    full = np.concatenate(rows, axis=0).astype(np.float32)
    high = full.astype(jnp.bfloat16)
    low = (full - high.astype(np.float32)).astype(jnp.bfloat16)
    return np.concatenate([high, high, low, high], axis=1)


def weight_table():
    fine = node_tables()[2]
    table = np.zeros((8, 8, LANES), np.float32)
    for target in range(8):
        others = [other for other in range(8) if other != target]
        scale = 1.0
        for j, other in enumerate(others):
            table[j, target] = fine[other]
            scale /= fine[target] - fine[other]
        table[7, target] = scale
    return table


DIRS = [
    (i, j, k)
    for size in (3, 2, 1)
    for i in (-1, 0, 1)
    for j in (-1, 0, 1)
    for k in (-1, 0, 1)
    if abs(i) + abs(j) + abs(k) == size
]


def slot_of(way):
    return (way[0] + 1) * 9 + (way[1] + 1) * 3 + way[2] + 1


def face_rows(way):
    x, y, z = (None if w == 0 else (3 if w > 0 else 0) for w in way)
    if x is not None and y is not None and z is not None:
        return [(16 * x + 4 * y + z, 1, 1)]
    if x is not None and y is not None:
        return [(16 * x + 4 * y, 4, 1)]
    if x is not None and z is not None:
        return [(16 * x + z, 4, 4)]
    if y is not None and z is not None:
        return [(4 * y + z, 4, 16)]
    if x is not None:
        return [(16 * x, 16, 1)]
    if y is not None:
        return [(16 * a + 4 * y, 4, 1) for a in range(4)]
    return [(z, 16, 4)]


def length_of(way):
    return sum(size for _, size, _ in face_rows(way))


def rows_of(piece):
    start, size, stride = piece
    return (pl.ds(start, size, stride=stride) if stride > 1 else pl.ds(start, size), slice(None))


def kernel(
    sizes,
    ops_hbm,
    load_hbm,
    trial_hbm,
    grad_hbm,
    table_hbm,
    coords_hbm,
    old_hbm,
    line_hbm,
    index_hbm,
    sol_hbm,
    vel_hbm,
    power_ref,
    flow_hbm,
    moved_hbm,
    sol_ref,
    vel,
    flow_ref,
    moved_ref,
    ops,
    load,
    trial,
    grad,
    table_ref,
    coords,
    old,
    host,
    index,
    pay_ref,
    old_ref,
    upd,
    res,
    wgt,
    img,
    work,
    face_out,
    face_in,
    pay_in,
    back_out,
    back_in,
    red_out,
    red_in,
    local_sem,
    face_send,
    face_recv,
    pay_send,
    pay_recv,
    back_send,
    back_recv,
    red_send,
    red_recv,
):
    me = [lax.axis_index(axis) for axis in AXES]
    line = sizes[0]
    plane = sizes[1] * sizes[2]
    groups = pay_ref.shape[1]

    pairs = [
        (ops_hbm, ops),
        (load_hbm, load),
        (line_hbm, host),
        (index_hbm, index),
        (coords_hbm, coords),
        (old_hbm, old),
        (table_hbm, table_ref),
        (trial_hbm, trial),
        (grad_hbm, grad),
    ]
    loads = [
        pltpu.make_async_copy(src, dst, local_sem.at[i]) for i, (src, dst) in enumerate(pairs)
    ]
    for copy in loads:
        copy.start()
    pairs = [(sol_ref, sol_hbm), (vel, vel_hbm), (flow_ref, flow_hbm), (moved_ref, moved_hbm)]
    stores = [
        pltpu.make_async_copy(src, dst, local_sem.at[9 + i]) for i, (src, dst) in enumerate(pairs)
    ]

    def edge(d, step):
        return me[d] < sizes[d] - 1 if step > 0 else me[d] > 0

    def exists(way):
        tests = [edge(d, way[d]) for d in range(3) if way[d] != 0]
        return functools.reduce(jnp.logical_and, tests)

    present = {way: exists(way) for way in DIRS}

    def beside(way):
        return {AXES[d]: me[d] + way[d] for d in range(3) if way[d] != 0}

    def along(offset):
        return {AXES[0]: lax.rem(me[0] + offset, sizes[0])}

    def across(offset):
        j, k = offset // sizes[2], offset % sizes[2]
        return {
            AXES[1]: lax.rem(me[1] + j, sizes[1]),
            AXES[2]: lax.rem(me[2] + k, sizes[2]),
        }

    barrier = pltpu.get_barrier_semaphore()
    partners = [along(offset) for offset in range(1, line)]
    partners += [across(offset) for offset in range(1, plane)]
    for partner in partners:
        pl.semaphore_signal(barrier, inc=1, device_id=partner, device_id_type=MESH)
    slanted = [way for way in DIRS if way[0] != 0 and (way[1] != 0 or way[2] != 0)]
    for way in slanted:

        @pl.when(present[way])
        def _():
            pl.semaphore_signal(barrier, inc=1, device_id=beside(way), device_id_type=MESH)

    for way in DIRS:

        @pl.when(jnp.logical_not(present[way]))
        def _():
            for x in range(SWEEPS + 1):
                face_in[x, slot_of(way)] = jnp.zeros((2 * FACE, LANES), jnp.float32)

    lane = lax.broadcasted_iota(jnp.int32, (40, LANES), 1)
    place = [lane // (EY * EZ), lane // EZ % EY, lane % EZ]

    def face_copy(x, way, parts):
        rows = max(8, parts * length_of(way))
        there = slot_of(tuple(-w for w in way))
        return pltpu.make_async_remote_copy(
            src_ref=face_out.at[x, slot_of(way), pl.ds(0, rows)],
            dst_ref=face_in.at[x, there, pl.ds(0, rows)],
            send_sem=face_send.at[x, slot_of(way)],
            recv_sem=face_recv.at[x, there],
            device_id=beside(way),
            device_id_type=MESH,
        )

    def open_faces(x, parts):
        for group in (DIRS[:8], DIRS[8:20], DIRS[20:]):
            for way in group:
                at = 0
                for ref in parts:
                    for piece in face_rows(way):
                        face_out[x, slot_of(way), at : at + piece[1]] = ref[rows_of(piece)]
                        at += piece[1]
            for way in group:

                @pl.when(present[way])
                def _():
                    face_copy(x, way, len(parts)).start()

    def combine(d, pieces):
        at = 0
        for size, *places in pieces:
            for s, (ref, piece) in enumerate(places):
                work[s, at : at + size] = ref[rows_of(piece)]
            at += size
        count, step = COUNTS[d], STEPS[d]
        far = (count - 1) * step
        total = -(-at // 8) * 8
        low, high, before, after = (work[s, 0:total] for s in range(4))
        where_at = place[d][0:total]
        new = (
            low
            + jnp.where(
                where_at > 0,
                pltpu.roll(high, step, 1),
                pltpu.roll(before, (LANES - far) % LANES, 1),
            ),
            high
            + jnp.where(
                where_at < count - 1,
                pltpu.roll(low, LANES - step, 1),
                pltpu.roll(after, far, 1),
            ),
        )
        at = 0
        for size, *places in pieces:
            for s in range(2):
                ref, piece = places[s]
                ref[rows_of(piece)] = new[s][at : at + size]
            at += size

    def close_faces(x, parts):
        for way in DIRS:

            @pl.when(present[way])
            def _():
                face_copy(x, tuple(-w for w in way), len(parts)).wait_recv()

        ends = (-1, 1)
        for p, ref in enumerate(parts):

            def got(way, start=0, size=None, stride=1):
                full = length_of(way)
                return (
                    face_in.at[x, slot_of(way)],
                    (p * full + start, full if size is None else size, stride),
                )

            pieces = [(16, (ref, (0, 16, 1)), (ref, (48, 16, 1)), got((-1, 0, 0)), got((1, 0, 0)))]
            for o in ends:
                for way in ((0, o, 0), (0, 0, o)):
                    lo, hi = (-1, *way[1:]), (1, *way[1:])
                    pieces.append((4, got(way, 0, 4), got(way, 12, 4), got(lo), got(hi)))
            for oy in ends:
                for oz in ends:
                    way = (0, oy, oz)
                    pieces.append(
                        (1, got(way, 0, 1), got(way, 3, 1), got((-1, oy, oz)), got((1, oy, oz)))
                    )
            combine(0, pieces)
            pieces = []
            for a in range(4):
                pieces.append(
                    (
                        4,
                        (ref, (16 * a, 4, 1)),
                        (ref, (16 * a + 12, 4, 1)),
                        got((0, -1, 0), 4 * a, 4),
                        got((0, 1, 0), 4 * a, 4),
                    )
                )
            for oz in ends:
                way = (0, 0, oz)
                pieces.append(
                    (4, got(way, 0, 4, 4), got(way, 3, 4, 4), got((0, -1, oz)), got((0, 1, oz)))
                )
            combine(1, pieces)
            combine(
                2,
                [(16, (ref, (0, 16, 4)), (ref, (3, 16, 4)), got((0, 0, -1)), got((0, 0, 1)))],
            )

    def apply_operator():
        def block(i, total):
            rows = upd[pl.ds(pl.multiple_of(8 * i, 8), 8), :]
            for j in range(8):
                total = total + ops[8 * i + j] * rows[j : j + 1, :]
            return total

        img[...] = lax.fori_loop(0, NODES // 8, block, jnp.zeros((NODES, LANES), jnp.float32))

    loads[0].wait()
    loads[1].wait()
    res[...] = load[...]
    for n in range(NODES):
        wgt[n : n + 1, :] = ops[n, n : n + 1, :]

    near = [sum(edge(d, step).astype(jnp.int32) for step in (-1, 1)) for d in range(3)]
    pl.semaphore_wait(barrier, len(partners) + near[0] * ((1 + near[1]) * (1 + near[2]) - 1))

    open_faces(0, (res, wgt))

    def pay_copy(offset):
        return pltpu.make_async_remote_copy(
            src_ref=pay_ref,
            dst_ref=pay_in.at[offset - 1],
            send_sem=pay_send.at[offset - 1],
            recv_sem=pay_recv.at[offset - 1],
            device_id=along(offset),
            device_id_type=MESH,
        )

    for copy in loads[2:]:
        copy.wait()
    pay_ref[3] = (host[...] * LANES + index[...]).astype(jnp.float32)
    for d in range(3):
        for g in range(groups):
            lanes = slice(g * LANES, (g + 1) * LANES)
            pay_ref[d, g : g + 1, :] = coords[d : d + 1, lanes]
            old_ref[d, g : g + 1, :] = old[d : d + 1, lanes]
    for offset in range(1, line):
        pay_copy(offset).start()
    close_faces(0, (res, wgt))

    center = 0.5 * (upper_bound + lower_bound)
    radius = 0.5 * (upper_bound - lower_bound)
    sigma = center / radius
    rho = 1.0 / sigma
    upd[...] = res[...] / (center * wgt[...])
    sol_ref[...] = upd[...]
    for sweep in range(SWEEPS - 1):
        apply_operator()
        open_faces(sweep + 1, (img,))
        close_faces(sweep + 1, (img,))
        left = res[...] - img[...]
        res[...] = left
        rho_next = 1.0 / (2.0 * sigma - rho)
        new = (rho_next * rho) * upd[...] + (2.0 * rho_next / radius) * left / wgt[...]
        rho = rho_next
        upd[...] = new
        sol_ref[...] = sol_ref[...] + new

    last = SWEEPS
    apply_operator()
    open_faces(last, (img,))

    pressure = sol_ref[...]
    p_high = pressure.astype(jnp.bfloat16)
    rest = pressure - p_high.astype(jnp.float32)
    p_mid = rest.astype(jnp.bfloat16)
    p_low = (rest - p_mid.astype(jnp.float32)).astype(jnp.bfloat16)
    pieces = jnp.concatenate([p_high, p_mid, p_high, p_low], axis=0)
    tile = FINE

    def correct(i, top):
        speed = jnp.zeros((tile, LANES), jnp.float32)
        for d in range(3):
            rows = pl.ds(pl.multiple_of(i * tile, tile), tile)
            slope = jnp.dot(grad[d, rows, :], pieces, preferred_element_type=jnp.float32)
            value = (trial[d, rows, :] - slope).astype(jnp.bfloat16)
            vel[d, rows, :] = value
            speed = speed + jnp.abs(value.astype(jnp.float32))
        return jnp.maximum(top, speed)

    top = lax.fori_loop(0, FINE // tile, correct, jnp.zeros((tile, LANES), jnp.float32))
    stores[0].start()
    stores[1].start()
    top = jnp.max(top.reshape(tile // 8, 8, LANES), axis=0)

    element = lax.broadcasted_iota(jnp.int32, (LANES, LANES), 0).astype(jnp.float32)
    own_first = (me[0] * LANES).astype(jnp.float32)

    def interpolate(source, target, first, end):
        def lagrange(point):
            value = table_ref[7]
            for j in range(7):
                value = value * (point - table_ref[j])
            return value

        def one_tile(i, carry):
            hot = []
            weights = []
            for h in range(2):
                row = pl.ds(2 * i + h, 1)
                key = source[3, row, :] - own_first
                hot.append(jnp.where(element == key, 1.0, 0.0).astype(jnp.bfloat16))
                weights.append([lagrange(source[axis, row, :]) for axis in range(3)])
            chosen = jnp.concatenate(hot, axis=1)
            for d in range(3):
                taken = jnp.dot(vel[d], chosen, preferred_element_type=jnp.float32)
                for h in range(2):
                    part = taken[:, h * LANES : (h + 1) * LANES]
                    w_x, w_y, w_z = weights[h]
                    over_x = w_x[0:1] * part[0:64]
                    for k in range(1, 8):
                        over_x = over_x + w_x[k : k + 1] * part[64 * k : 64 * k + 64]
                    over_y = w_y[0:1] * over_x[0:8]
                    for l in range(1, 8):
                        over_y = over_y + w_y[l : l + 1] * over_x[8 * l : 8 * l + 8]
                    target[d, pl.ds(2 * i + h, 1), :] = jnp.sum(
                        w_z * over_y, axis=0, keepdims=True
                    )
            return carry

        lax.fori_loop(first, end, one_tile, 0)

    def back_copy(offset):
        return pltpu.make_async_remote_copy(
            src_ref=back_out.at[offset],
            dst_ref=back_in.at[line - offset - 1],
            send_sem=back_send.at[offset],
            recv_sem=back_recv.at[line - offset - 1],
            device_id=along(offset),
            device_id_type=MESH,
        )

    spans = (plane, line)
    bases = (0, plane)
    mine = (me[1] * sizes[2] + me[2], me[0])

    def red_copy(d, offset):
        return pltpu.make_async_remote_copy(
            src_ref=red_out.at[d],
            dst_ref=red_in.at[bases[d] + mine[d]],
            send_sem=red_send.at[bases[d] + offset],
            recv_sem=red_recv.at[bases[d] + offset],
            device_id=along(offset) if d else across(offset),
            device_id_type=MESH,
        )

    def open_sums(d, value):
        red_out[d] = value
        for offset in range(1, spans[d]):
            red_copy(d, offset).start()
        red_in[bases[d] + mine[d]] = value

    def close_sums(d):
        for offset in range(1, spans[d]):
            red_copy(d, offset).wait_recv()
        most, total = red_in[bases[d], 0:8], red_in[bases[d], 8:16]
        for i in range(1, spans[d]):
            most = jnp.maximum(most, red_in[bases[d] + i, 0:8])
            total = total + red_in[bases[d] + i, 8:16]
        return jnp.concatenate([most, total], axis=0)

    def finish_faces():
        close_faces(last, (img,))
        left = res[...] - img[...]
        squares = jnp.sum((left * left).reshape(NODES // 8, 8, LANES), axis=0)
        open_sums(0, jnp.concatenate([top, squares], axis=0))

    def finish_plane():
        open_sums(1, close_sums(0))

    todo = {2: finish_faces, 4: finish_plane}
    tiles = groups // 2
    half = tiles // 2
    turn = 0
    for offset in range(1, line):
        pay_copy(offset).wait_recv()
        slot = line - offset
        for first, end in ((0, half), (half, tiles)):
            interpolate(pay_in.at[offset - 1], back_out.at[slot], first, end)
            if end == tiles:
                back_copy(slot).start()
            if turn in todo:
                todo.pop(turn)()
            turn += 1
    for turn in sorted(todo):
        todo[turn]()
    interpolate(pay_ref, back_out.at[0], 0, tiles)

    value = close_sums(1)
    largest = jnp.max(value[0:8])
    power_ref[0, 0] = jnp.sum(value[8:16]) * (
        1.0 / (float(NODES * LANES) * sizes[0] * sizes[1] * sizes[2])
    )
    stride = courant / (jnp.full((groups, LANES), largest, jnp.float32) + 1e-06)
    for offset in range(1, line):
        back_copy(offset).wait_recv()
    for d in range(3):
        flow = back_out[0, d]
        for offset in range(1, line):
            flow = flow + back_in[offset - 1, d]
        moved = pay_ref[d] + stride * (1.5 * flow - 0.5 * old_ref[d])
        for g in range(groups):
            flow_ref[d : d + 1, g * LANES : (g + 1) * LANES] = flow[g : g + 1]
            moved_ref[d : d + 1, g * LANES : (g + 1) * LANES] = moved[g : g + 1]

    stores[2].start()
    stores[3].start()
    for offset in range(1, line):
        pay_copy(offset).wait_send()
        back_copy(offset).wait_send()
    for d in range(2):
        for offset in range(1, spans[d]):
            red_copy(d, offset).wait_send()
    for way in DIRS:

        @pl.when(present[way])
        def _():
            for x in range(SWEEPS + 1):
                face_copy(x, way, 2 if x == 0 else 1).wait_send()

    for copy in stores:
        copy.wait()


def write_out(*refs):
    count = (len(refs) - 2) // 3
    sources, targets, held = refs[:count], refs[count : 2 * count], refs[2 * count : 3 * count]
    taken, given = refs[3 * count :]
    inward = [pltpu.make_async_copy(sources[i], held[i], taken.at[i]) for i in range(count)]
    outward = [pltpu.make_async_copy(held[i], targets[i], given.at[i]) for i in range(count)]
    for copy in inward:
        copy.start()
    for i in range(count):
        inward[i].wait()
        outward[i].start()
    for copy in outward:
        copy.wait()


def per_device(
    sizes,
    element_ops,
    load_terms,
    trial_velocity,
    tracer_coords,
    tracer_old_velocity,
    host_line,
    host_element_index,
):
    count = host_element_index.shape[0]
    groups = count // LANES
    line = sizes[0]
    matrix = jnp.asarray(gradient_matrix()).reshape(3, FINE, 4 * NODES)
    f32 = jnp.float32
    i32 = jnp.int32
    bf16 = jnp.bfloat16
    hbm = pl.BlockSpec(memory_space=pl.ANY)
    links = line + sizes[1] * sizes[2]
    dma = pltpu.SemaphoreType.DMA
    small = [pltpu.VMEM((NODES, LANES), f32)] * 4
    solution, velocity, power, flows, moved = pl.pallas_call(
        functools.partial(kernel, sizes),
        out_shape=(
            jax.ShapeDtypeStruct((NODES, LANES), f32),
            jax.ShapeDtypeStruct((3, FINE, LANES), bf16),
            jax.ShapeDtypeStruct((1, 1), f32),
            jax.ShapeDtypeStruct((3, count), f32),
            jax.ShapeDtypeStruct((3, count), f32),
        ),
        in_specs=[hbm] * 9,
        out_specs=(hbm, hbm, pl.BlockSpec(memory_space=pltpu.SMEM), hbm, hbm),
        scratch_shapes=[
            pltpu.VMEM((NODES, LANES), f32),
            pltpu.VMEM((3, FINE, LANES), bf16),
            pltpu.VMEM((3, count), f32),
            pltpu.VMEM((3, count), f32),
            pltpu.VMEM((NODES, NODES, LANES), f32),
            pltpu.VMEM((NODES, LANES), f32),
            pltpu.VMEM((3, FINE, LANES), f32),
            pltpu.VMEM((3, FINE, 4 * NODES), bf16),
            pltpu.VMEM((8, 8, LANES), f32),
            pltpu.VMEM((3, count), f32),
            pltpu.VMEM((3, count), f32),
            pltpu.VMEM((groups, LANES), i32),
            pltpu.VMEM((groups, LANES), i32),
            pltpu.VMEM((4, groups, LANES), f32),
            pltpu.VMEM((3, groups, LANES), f32),
            *small,
            pltpu.VMEM((4, 40, LANES), f32),
            pltpu.VMEM((SWEEPS + 1, 27, 2 * FACE, LANES), f32),
            pltpu.VMEM((SWEEPS + 1, 27, 2 * FACE, LANES), f32),
            pltpu.VMEM((line - 1, 4, groups, LANES), f32),
            pltpu.VMEM((line, 3, groups, LANES), f32),
            pltpu.VMEM((line - 1, 3, groups, LANES), f32),
            pltpu.VMEM((2, 16, LANES), f32),
            pltpu.VMEM((links, 16, LANES), f32),
            dma((13,)),
            dma((SWEEPS + 1, 27)),
            dma((SWEEPS + 1, 27)),
            dma((line - 1,)),
            dma((line - 1,)),
            dma((line,)),
            dma((line,)),
            dma((links,)),
            dma((links,)),
        ],
        compiler_params=pltpu.CompilerParams(
            collective_id=0, has_side_effects=True
        ),
        name="brick",
    )(
        element_ops,
        load_terms,
        trial_velocity,
        matrix,
        jnp.asarray(weight_table()),
        tracer_coords,
        tracer_old_velocity,
        host_line.reshape(groups, LANES),
        host_element_index.reshape(groups, LANES),
    )
    results = (solution, velocity, flows, moved)
    solution, velocity, flows, moved = pl.pallas_call(
        write_out,
        out_shape=tuple(jax.ShapeDtypeStruct(r.shape, r.dtype) for r in results),
        in_specs=[hbm] * 4,
        out_specs=(hbm,) * 4,
        scratch_shapes=[pltpu.VMEM(r.shape, r.dtype) for r in results] + [dma((4,)), dma((4,))],
        name="write_out",
    )(*results)
    return (solution, velocity, power[0, 0], flows, moved)


def solution(mesh):
    sizes = tuple(mesh.shape[axis] for axis in AXES)
    placed = (
        P(None, None, AXES),
        P(None, AXES),
        P(None, None, AXES),
        P(None, AXES),
        P(None, AXES),
        P(AXES, None),
        P(AXES),
    )
    return jax.shard_map(
        functools.partial(per_device, sizes),
        mesh=mesh,
        in_specs=placed,
        out_specs=(
            P(None, AXES),
            P(None, None, AXES),
            P(),
            P(None, AXES),
            P(None, AXES),
        ),
        check_vma=False,
    )
```

profile of v0, /device:TPU:0, one launch (start us, length us, event | category | flops | bytes accessed | tf_op | source)
XLA Modules:
  0.0 43.7 jit_solution(12564208153965866415)
XLA Ops:
  0.6 39.4 %brick.1 = (f32[64,128]{1,0:T(8,128)}, bf16[3,512,128]{2,1,0:T(8,128)(2,1)}, f32[1,1]{1,0:T(1,128)}, f32[3,2048]{1,0:T(4,128)}, f32[3,2048]{1,0:T(4,128)}) custom-call(f32[64,64,128]{2,1,0:T(8,128)} %ops_hbm.1, f32[64,128]{1,0:T(8,128)} %load_hbm.1, f32[3,512,128]{2,1,0:T(8,128)} %trial_hbm.1, bf16[3,512,256]{2,1,0:T(8,128)(2,1)} %constant.6.grad_hbm, ...), custom_call_target="tpu_custom_call" | custom-call | tf_op jit(solution)/shard_map/brick/pallas_call | solution.py:612
  40.1 1.8 %write_out.1 = (f32[64,128]{1,0:T(8,128)}, bf16[3,512,128]{2,1,0:T(8,128)(2,1)}, f32[3,2048]{1,0:T(4,128)}, f32[3,2048]{1,0:T(4,128)}) custom-call(f32[64,128]{1,0:T(8,128)} %get-tuple-element.14.refs_0_, bf16[3,512,128]{2,1,0:T(8,128)(2,1)} %get-tuple-element.15.refs_1_, f32[3,2048]{1,0:T(4,128)} %get-tuple-element.16.refs_2_, ...), custom_call_target="tpu_custom_call" | custom-call | tf_op jit(solution)/shard_map/write_out/pallas_call | solution.py:674
where the time goes:
time: 43.9 us; the launch traced here: 43.7 us
  Pallas kernels  41.3 us (94%)
  between operations  2.46 us (6%)
    pallas_call x1, Pallas kernels, per_device(): pl.pallas_call(functools.partial(kernel, sizes), out_shape=(jax.ShapeDtyp...  39.4 us
    pallas_call x1, Pallas kernels, per_device(): pl.pallas_call(write_out, out_shape=tuple((jax.ShapeDtypeStruct(r.shape,...  1.84 us

commit v1 on v0

v1 whole, which is shorter than its diff:
```python
import functools

import jax
import jax.numpy as jnp
import numpy as np
from jax import lax
from jax.experimental import pallas as pl
from jax.experimental.pallas import tpu as pltpu
from jax.sharding import PartitionSpec as P

EX = 4
EY = 4
EZ = 8
SWEEPS = 4
NODES = 64
FACE = 16
LANES = 128
FINE = 512

lower_bound = 0.25
upper_bound = 2.0
courant = 0.5
AXES = ("gx", "gy", "gz")
COUNTS = (EX, EY, EZ)
STEPS = (EY * EZ, EZ, 1)
MESH = pl.DeviceIdType.MESH
FINISH = 4
BRICK_VMEM = 24 * 1024 * 1024
OUT_VMEM = 4 * 1024 * 1024


def node_tables():
    coarse = -np.cos(np.pi * np.arange(4) / 3.0)
    fine = -np.cos(np.pi * np.arange(8) / 7.0)
    plain = np.zeros((8, 4))
    slope = np.zeros((8, 4))
    for target in range(8):
        for source in range(4):
            others = [other for other in range(4) if other != source]
            value = 1.0
            for other in others:
                value *= (fine[target] - coarse[other]) / (coarse[source] - coarse[other])
            plain[target, source] = value
            total = 0.0
            for skipped in others:
                term = 1.0 / (coarse[source] - coarse[skipped])
                for other in others:
                    if other != skipped:
                        term *= (fine[target] - coarse[other]) / (coarse[source] - coarse[other])
                total += term
            slope[target, source] = total
    return plain, slope, fine


def gradient_matrix():
    plain, slope, _ = node_tables()
    rows = [
        np.kron(np.kron(slope, plain), plain),
        np.kron(np.kron(plain, slope), plain),
        np.kron(np.kron(plain, plain), slope),
    ]
    full = np.concatenate(rows, axis=0).astype(np.float32)
    high = full.astype(jnp.bfloat16)
    low = (full - high.astype(np.float32)).astype(jnp.bfloat16)
    return np.concatenate([high, high, low, high], axis=1)


def weight_table():
    fine = node_tables()[2]
    table = np.zeros((8, 8, LANES), np.float32)
    for target in range(8):
        others = [other for other in range(8) if other != target]
        scale = 1.0
        for j, other in enumerate(others):
            table[j, target] = fine[other]
            scale /= fine[target] - fine[other]
        table[7, target] = scale
    return table


DIRS = [
    (i, j, k)
    for size in (3, 2, 1)
    for i in (-1, 0, 1)
    for j in (-1, 0, 1)
    for k in (-1, 0, 1)
    if abs(i) + abs(j) + abs(k) == size
]


def slot_of(way):
    return (way[0] + 1) * 9 + (way[1] + 1) * 3 + way[2] + 1


def face_rows(way):
    x, y, z = (None if w == 0 else (3 if w > 0 else 0) for w in way)
    if x is not None and y is not None and z is not None:
        return [(16 * x + 4 * y + z, 1, 1)]
    if x is not None and y is not None:
        return [(16 * x + 4 * y, 4, 1)]
    if x is not None and z is not None:
        return [(16 * x + z, 4, 4)]
    if y is not None and z is not None:
        return [(4 * y + z, 4, 16)]
    if x is not None:
        return [(16 * x, 16, 1)]
    if y is not None:
        return [(16 * a + 4 * y, 4, 1) for a in range(4)]
    return [(z, 16, 4)]


def length_of(way):
    return sum(size for _, size, _ in face_rows(way))


def rows_of(piece):
    start, size, stride = piece
    return (pl.ds(start, size, stride=stride) if stride > 1 else pl.ds(start, size), slice(None))


def bit_moves(size):
    return [1 << bit for bit in range(size.bit_length()) if 1 << bit < size]


def kernel(
    sizes,
    direct,
    ops_hbm,
    load_hbm,
    trial_hbm,
    grad_hbm,
    table_hbm,
    coords_hbm,
    old_hbm,
    line_hbm,
    index_hbm,
    sol_ref,
    vel,
    power_ref,
    flow_ref,
    moved_ref,
    ops,
    load,
    trial,
    grad,
    table_ref,
    coords,
    old,
    host,
    index,
    pay_ref,
    old_ref,
    upd,
    res,
    wgt,
    img,
    work,
    wide,
    face_out,
    face_in,
    pay_in,
    back_out,
    back_in,
    red_out,
    red_in,
    local_sem,
    face_send,
    face_recv,
    pay_send,
    pay_recv,
    back_send,
    back_recv,
    red_send,
    red_recv,
):
    me = [lax.axis_index(axis) for axis in AXES]
    line = sizes[0]
    groups = pay_ref.shape[1]

    def edge(d, step):
        return me[d] < sizes[d] - 1 if step > 0 else me[d] > 0

    def exists(way):
        tests = [edge(d, way[d]) for d in range(3) if way[d] != 0]
        return functools.reduce(jnp.logical_and, tests)

    present = {way: exists(way) for way in DIRS}

    def beside(way):
        return {AXES[d]: me[d] + way[d] for d in range(3) if way[d] != 0}

    def along(offset):
        there = me[0]
        for bit in bit_moves(line):
            if offset & bit:
                there = there + bit * (1 - 2 * lax.rem(me[0] // bit, 2))
        return {AXES[0]: there}

    def shifted(offset):
        return {
            AXES[d]: lax.rem(me[d] + offset[d], sizes[d]) for d in range(3) if offset[d] != 0
        }

    spans = [range(size) for size in sizes]
    if direct:
        teams = [[(i, j, k) for i in spans[0] for j in spans[1] for k in spans[2]]]
        seats = [(me[0] * sizes[1] + me[1]) * sizes[2] + me[2]]
    else:
        teams = [[(0, j, k) for j in spans[1] for k in spans[2]], [(i, 0, 0) for i in spans[0]]]
        seats = [me[1] * sizes[2] + me[2], me[0]]
    bases = [sum(len(team) for team in teams[:t]) for t in range(len(teams))]

    barrier = pltpu.get_barrier_semaphore()
    for way in DIRS:

        @pl.when(present[way])
        def _():
            pl.semaphore_signal(barrier, inc=1, device_id=beside(way), device_id_type=MESH)

    partners = [along(offset) for offset in range(1, line)]
    if not direct:
        partners += [shifted(offset) for team in teams for offset in team[1:]]
    for partner in partners:
        pl.semaphore_signal(barrier, inc=1, device_id=partner, device_id_type=MESH)

    pairs = [
        (ops_hbm, ops),
        (load_hbm, load),
        (line_hbm, host),
        (index_hbm, index),
        (coords_hbm, coords),
        (old_hbm, old),
        (table_hbm, table_ref),
        (trial_hbm, trial),
        (grad_hbm, grad),
    ]
    loads = [
        pltpu.make_async_copy(src, dst, local_sem.at[i]) for i, (src, dst) in enumerate(pairs)
    ]
    for i in (1, 0, 2, 3, 4, 5, 6, 7, 8):
        loads[i].start()

    for way in DIRS:

        @pl.when(jnp.logical_not(present[way]))
        def _():
            for x in range(SWEEPS + 1):
                face_in[x, slot_of(way)] = jnp.zeros((2 * FACE, LANES), jnp.float32)

    lane = lax.broadcasted_iota(jnp.int32, (40, LANES), 1)
    place = [lane // (EY * EZ), lane // EZ % EY, lane % EZ]

    def parts_of(x):
        return 2 if x == 0 else 1

    def face_copy(x, way):
        rows = parts_of(x) * length_of(way)
        there = slot_of(tuple(-w for w in way))
        return pltpu.make_async_remote_copy(
            src_ref=face_out.at[x, slot_of(way), pl.ds(0, rows)],
            dst_ref=face_in.at[x, there, pl.ds(0, rows)],
            send_sem=face_send.at[x, slot_of(way)],
            recv_sem=face_recv.at[x, there],
            device_id=beside(way),
            device_id_type=MESH,
        )

    def fill_faces(x, parts, ways):
        for way in ways:
            at = 0
            for ref in parts:
                for piece in face_rows(way):
                    face_out[x, slot_of(way), at : at + piece[1]] = ref[rows_of(piece)]
                    at += piece[1]

    def start_faces(x, ways):
        for way in ways:

            @pl.when(present[way])
            def _():
                face_copy(x, way).start()

    def drain_faces(x):
        for way in DIRS:

            @pl.when(present[way])
            def _():
                face_copy(x, way).wait_send()

    def open_faces(x, parts):
        for group in (DIRS[:8], DIRS[8:20], DIRS[20:]):
            fill_faces(x, parts, group)
            start_faces(x, group)

    def combine(d, pieces):
        at = 0
        for size, *places in pieces:
            for s, (ref, piece) in enumerate(places):
                work[s, at : at + size] = ref[rows_of(piece)]
            at += size
        count, step = COUNTS[d], STEPS[d]
        far = (count - 1) * step
        total = -(-at // 8) * 8
        low, high, before, after = (work[s, 0:total] for s in range(4))
        where_at = place[d][0:total]
        new = (
            low
            + jnp.where(
                where_at > 0,
                pltpu.roll(high, step, 1),
                pltpu.roll(before, (LANES - far) % LANES, 1),
            ),
            high
            + jnp.where(
                where_at < count - 1,
                pltpu.roll(low, LANES - step, 1),
                pltpu.roll(after, far, 1),
            ),
        )
        at = 0
        for size, *places in pieces:
            for s in range(2):
                ref, piece = places[s]
                ref[rows_of(piece)] = new[s][at : at + size]
            at += size

    def close_faces(x, parts):
        for way in DIRS:

            @pl.when(present[way])
            def _():
                face_copy(x, tuple(-w for w in way)).wait_recv()

        ends = (-1, 1)
        for p, ref in enumerate(parts):

            def got(way, start=0, size=None, stride=1):
                full = length_of(way)
                return (
                    face_in.at[x, slot_of(way)],
                    (p * full + start, full if size is None else size, stride),
                )

            pieces = [(16, (ref, (0, 16, 1)), (ref, (48, 16, 1)), got((-1, 0, 0)), got((1, 0, 0)))]
            for o in ends:
                for way in ((0, o, 0), (0, 0, o)):
                    lo, hi = (-1, *way[1:]), (1, *way[1:])
                    pieces.append((4, got(way, 0, 4), got(way, 12, 4), got(lo), got(hi)))
            for oy in ends:
                for oz in ends:
                    way = (0, oy, oz)
                    pieces.append(
                        (1, got(way, 0, 1), got(way, 3, 1), got((-1, oy, oz)), got((1, oy, oz)))
                    )
            combine(0, pieces)
            pieces = []
            for a in range(4):
                pieces.append(
                    (
                        4,
                        (ref, (16 * a, 4, 1)),
                        (ref, (16 * a + 12, 4, 1)),
                        got((0, -1, 0), 4 * a, 4),
                        got((0, 1, 0), 4 * a, 4),
                    )
                )
            for oz in ends:
                way = (0, 0, oz)
                pieces.append(
                    (4, got(way, 0, 4, 4), got(way, 3, 4, 4), got((0, -1, oz)), got((0, 1, oz)))
                )
            combine(1, pieces)
            combine(
                2,
                [(16, (ref, (0, 16, 4)), (ref, (3, 16, 4)), got((0, 0, -1)), got((0, 0, 1)))],
            )

    def apply_operator():
        def block(i, total):
            rows = upd[pl.ds(pl.multiple_of(8 * i, 8), 8), :]
            for j in range(8):
                total = total + ops[8 * i + j] * rows[j : j + 1, :]
            return total

        img[...] = lax.fori_loop(0, NODES // 8, block, jnp.zeros((NODES, LANES), jnp.float32))

    def pay_copy(offset):
        return pltpu.make_async_remote_copy(
            src_ref=pay_ref,
            dst_ref=pay_in.at[offset - 1],
            send_sem=pay_send.at[offset - 1],
            recv_sem=pay_recv.at[offset - 1],
            device_id=along(offset),
            device_id_type=MESH,
        )

    def back_copy(offset):
        return pltpu.make_async_remote_copy(
            src_ref=back_out.at[offset],
            dst_ref=back_in.at[offset - 1],
            send_sem=back_send.at[offset - 1],
            recv_sem=back_recv.at[offset - 1],
            device_id=along(offset),
            device_id_type=MESH,
        )

    def red_copy(kind, t, offset):
        return pltpu.make_async_remote_copy(
            src_ref=red_out.at[kind, t, pl.ds(0, 1)],
            dst_ref=red_in.at[kind, bases[t] + seats[t], pl.ds(0, 1)],
            send_sem=red_send.at[kind, bases[t] + offset],
            recv_sem=red_recv.at[kind, bases[t] + offset],
            device_id=shifted(teams[t][offset]),
            device_id_type=MESH,
        )

    def open_sums(kind, t, value):
        red_out[kind, t, 0:1] = value
        for offset in range(len(teams[t]) - 1, 0, -1):
            red_copy(kind, t, offset).start()
        red_in[kind, bases[t] + seats[t], 0:1] = value

    def close_sums(kind, t):
        for offset in range(1, len(teams[t])):
            red_copy(kind, t, offset).wait_recv()
        values = [red_in[kind, bases[t] + i, 0:1] for i in range(len(teams[t]))]
        join = jnp.add if kind else jnp.maximum
        while len(values) > 1:
            values = [
                join(*values[i : i + 2]) if i + 1 < len(values) else values[i]
                for i in range(0, len(values), 2)
            ]
        return values[0]

    def drain_sums(kind):
        for t, team in enumerate(teams):
            for offset in range(1, len(team)):
                red_copy(kind, t, offset).wait_send()

    loads[1].wait()
    loads[0].wait()
    res[...] = load[...]
    for n in range(NODES):
        wgt[n : n + 1, :] = ops[n, n : n + 1, :]
    fill_faces(0, (res, wgt), DIRS)
    for copy in loads[2:7]:
        copy.wait()
    pay_ref[3] = (host[...] * LANES + index[...]).astype(jnp.float32)
    for d in range(3):
        for g in range(groups):
            lanes = slice(g * LANES, (g + 1) * LANES)
            pay_ref[d, g : g + 1, :] = coords[d : d + 1, lanes]
            old_ref[d, g : g + 1, :] = old[d : d + 1, lanes]

    near = [sum(edge(d, step).astype(jnp.int32) for step in (-1, 1)) for d in range(3)]
    pl.semaphore_wait(
        barrier, len(partners) + (1 + near[0]) * (1 + near[1]) * (1 + near[2]) - 1
    )

    start_faces(0, DIRS)
    order = range(line - 1, 0, -1)
    for offset in order:
        pay_copy(offset).start()
    close_faces(0, (res, wgt))

    center = 0.5 * (upper_bound + lower_bound)
    radius = 0.5 * (upper_bound - lower_bound)
    sigma = center / radius
    rho = 1.0 / sigma
    upd[...] = res[...] / (center * wgt[...])
    sol_ref[...] = upd[...]
    for sweep in range(SWEEPS - 1):
        apply_operator()
        open_faces(sweep + 1, (img,))
        drain_faces(sweep)
        if sweep + 2 == SWEEPS:
            for copy in loads[7:]:
                copy.wait()
            for offset in order:
                pay_copy(offset).wait_send()
        close_faces(sweep + 1, (img,))
        left = res[...] - img[...]
        res[...] = left
        rho_next = 1.0 / (2.0 * sigma - rho)
        new = (rho_next * rho) * upd[...] + (2.0 * rho_next / radius) * left / wgt[...]
        rho = rho_next
        upd[...] = new
        sol_ref[...] = sol_ref[...] + new

    last = SWEEPS
    apply_operator()
    open_faces(last, (img,))

    pressure = sol_ref[...]
    p_high = pressure.astype(jnp.bfloat16)
    rest = pressure - p_high.astype(jnp.float32)
    p_mid = rest.astype(jnp.bfloat16)
    p_low = (rest - p_mid.astype(jnp.float32)).astype(jnp.bfloat16)
    pieces = jnp.concatenate([p_high, p_mid, p_high, p_low], axis=0)
    speed = jnp.zeros((FINE, LANES), jnp.float32)
    for d in range(3):
        slope = jnp.dot(grad[d], pieces, preferred_element_type=jnp.float32)
        value = (trial[d] - slope).astype(jnp.bfloat16)
        vel[d] = value
        for k in range(8):
            wide[64 * d : 64 * d + 64, LANES * k : LANES * (k + 1)] = value[64 * k : 64 * k + 64]
        speed = speed + jnp.abs(value.astype(jnp.float32))
    open_sums(0, 0, jnp.max(speed, axis=0, keepdims=True))

    element = lax.broadcasted_iota(jnp.int32, (LANES, LANES), 0).astype(jnp.float32)
    own_first = (me[0] * LANES).astype(jnp.float32)

    def interpolate(source, target, first, end):
        def lagrange(point):
            value = table_ref[7]
            for j in range(7):
                value = value * (point - table_ref[j])
            return value

        def spread(row):
            row = jnp.broadcast_to(row, (16, LANES)).astype(jnp.bfloat16)
            return jnp.concatenate([row] * (LANES // 16), axis=0)

        def one_tile(i, carry):
            chosen = []
            weights = []
            for h in range(2):
                row = pl.ds(2 * i + h, 1)
                key = source[3, row, :] - own_first
                hot = jnp.where(element == key, 1.0, 0.0).astype(jnp.bfloat16)
                w_x, w_y, w_z = (lagrange(source[axis, row, :]) for axis in range(3))
                weights.append((w_y, w_z))
                chosen.append(
                    jnp.concatenate([hot * spread(w_x[k : k + 1]) for k in range(8)], axis=0)
                )
            taken = jnp.dot(
                wide[...],
                jnp.concatenate(chosen, axis=1),
                preferred_element_type=jnp.float32,
            )
            for d in range(3):
                for h in range(2):
                    part = taken[64 * d : 64 * d + 64, h * LANES : (h + 1) * LANES]
                    w_y, w_z = weights[h]
                    over_y = w_y[0:1] * part[0:8]
                    for l in range(1, 8):
                        over_y = over_y + w_y[l : l + 1] * part[8 * l : 8 * l + 8]
                    target[d, pl.ds(2 * i + h, 1), :] = jnp.sum(
                        w_z * over_y, axis=0, keepdims=True
                    )
            return carry

        lax.fori_loop(first, end, one_tile, 0)

    def finish_faces():
        drain_faces(last - 1)
        close_faces(last, (img,))
        left = res[...] - img[...]
        open_sums(1, 0, jnp.sum(left * left, axis=0, keepdims=True))

    tiles = groups // 2
    half = tiles // 2
    turn = 0
    for offset in order:
        pay_copy(offset).wait_recv()
        for first, end in ((0, half), (half, tiles)):
            interpolate(pay_in.at[offset - 1], back_out.at[offset], first, end)
            if end == tiles:
                back_copy(offset).start()
            turn += 1
            if turn == FINISH:
                finish_faces()
    if turn < FINISH:
        finish_faces()
    interpolate(pay_ref, back_out.at[0], 0, tiles)

    drain_faces(last)
    most = close_sums(0, 0)
    for t in range(1, len(teams)):
        open_sums(0, t, most)
        open_sums(1, t, close_sums(1, t - 1))
        most = close_sums(0, t)
    stride = courant / (jnp.max(most, axis=1, keepdims=True) + 1e-06)
    stride = jnp.broadcast_to(stride, (groups, LANES))
    drain_sums(0)
    for offset in order:
        back_copy(offset).wait_send()
    for offset in order:
        back_copy(offset).wait_recv()
    for d in range(3):
        flow = back_out[0, d]
        for offset in range(1, line):
            flow = flow + back_in[offset - 1, d]
        moved = pay_ref[d] + stride * (1.5 * flow - 0.5 * old_ref[d])
        for g in range(groups):
            flow_ref[d : d + 1, g * LANES : (g + 1) * LANES] = flow[g : g + 1]
            moved_ref[d : d + 1, g * LANES : (g + 1) * LANES] = moved[g : g + 1]

    power_ref[0, 0] = jnp.sum(close_sums(1, len(teams) - 1)) * (
        1.0 / (float(NODES * LANES) * sizes[0] * sizes[1] * sizes[2])
    )
    drain_sums(1)


def write_out(*refs):
    count = (len(refs) - 1) // 2
    sources, targets, given = refs[:count], refs[count : 2 * count], refs[2 * count]
    outward = [pltpu.make_async_copy(sources[i], targets[i], given.at[i]) for i in range(count)]
    for copy in outward:
        copy.start()
    for copy in outward:
        copy.wait()


def per_device(
    sizes,
    element_ops,
    load_terms,
    trial_velocity,
    tracer_coords,
    tracer_old_velocity,
    host_line,
    host_element_index,
):
    count = host_element_index.shape[0]
    groups = count // LANES
    line = sizes[0]
    direct = max(sizes) <= SWEEPS
    seats = sizes[0] * sizes[1] * sizes[2] if direct else sizes[0] + sizes[1] * sizes[2]
    matrix = jnp.asarray(gradient_matrix()).reshape(3, FINE, 4 * NODES)
    f32 = jnp.float32
    i32 = jnp.int32
    bf16 = jnp.bfloat16
    hbm = pl.BlockSpec(memory_space=pltpu.HBM)
    vmem = pl.BlockSpec(memory_space=pltpu.VMEM)
    dma = pltpu.SemaphoreType.DMA
    small = [pltpu.VMEM((NODES, LANES), f32)] * 4
    operands = (
        element_ops,
        load_terms,
        trial_velocity,
        matrix,
        jnp.asarray(weight_table()),
        tracer_coords,
        tracer_old_velocity,
        host_line.reshape(groups, LANES),
        host_element_index.reshape(groups, LANES),
    )
    solution, velocity, power, flows, moved = pl.pallas_call(
        functools.partial(kernel, sizes, direct),
        out_shape=(
            pltpu.VMEM((NODES, LANES), f32),
            pltpu.VMEM((3, FINE, LANES), bf16),
            jax.ShapeDtypeStruct((1, 1), f32),
            pltpu.VMEM((3, count), f32),
            pltpu.VMEM((3, count), f32),
        ),
        in_specs=[hbm] * 9,
        out_specs=(vmem, vmem, pl.BlockSpec(memory_space=pltpu.SMEM), vmem, vmem),
        scratch_shapes=[
            pltpu.VMEM((NODES, NODES, LANES), f32),
            pltpu.VMEM((NODES, LANES), f32),
            pltpu.VMEM((3, FINE, LANES), f32),
            pltpu.VMEM((3, FINE, 4 * NODES), bf16),
            pltpu.VMEM((8, 8, LANES), f32),
            pltpu.VMEM((3, count), f32),
            pltpu.VMEM((3, count), f32),
            pltpu.VMEM((groups, LANES), i32),
            pltpu.VMEM((groups, LANES), i32),
            pltpu.VMEM((4, groups, LANES), f32),
            pltpu.VMEM((3, groups, LANES), f32),
            *small,
            pltpu.VMEM((4, 40, LANES), f32),
            pltpu.VMEM((3 * NODES, 8 * LANES), bf16),
            pltpu.VMEM((SWEEPS + 1, 27, 2 * FACE, LANES), f32),
            pltpu.VMEM((SWEEPS + 1, 27, 2 * FACE, LANES), f32),
            pltpu.VMEM((line - 1, 4, groups, LANES), f32),
            pltpu.VMEM((line, 3, groups, LANES), f32),
            pltpu.VMEM((line - 1, 3, groups, LANES), f32),
            pltpu.VMEM((2, 2, 8, LANES), f32),
            pltpu.VMEM((2, seats, 8, LANES), f32),
            dma((9,)),
            dma((SWEEPS + 1, 27)),
            dma((SWEEPS + 1, 27)),
            dma((line - 1,)),
            dma((line - 1,)),
            dma((line - 1,)),
            dma((line - 1,)),
            dma((2, seats)),
            dma((2, seats)),
        ],
        compiler_params=pltpu.CompilerParams(
            collective_id=0, has_side_effects=True, vmem_limit_bytes=BRICK_VMEM
        ),
        name="brick",
    )(*(pltpu.with_memory_space_constraint(operand, pltpu.HBM) for operand in operands))
    results = (solution, velocity, flows, moved)
    solution, velocity, flows, moved = pl.pallas_call(
        write_out,
        out_shape=tuple(jax.ShapeDtypeStruct(r.shape, r.dtype) for r in results),
        in_specs=[pl.BlockSpec(memory_space=pl.ANY)] * 4,
        out_specs=(hbm,) * 4,
        scratch_shapes=[dma((4,))],
        compiler_params=pltpu.CompilerParams(vmem_limit_bytes=OUT_VMEM),
        name="write_out",
    )(*results)
    return (solution, velocity, power[0, 0], flows, moved)


def solution(mesh):
    sizes = tuple(mesh.shape[axis] for axis in AXES)
    placed = (
        P(None, None, AXES),
        P(None, AXES),
        P(None, None, AXES),
        P(None, AXES),
        P(None, AXES),
        P(AXES, None),
        P(AXES),
    )
    return jax.shard_map(
        functools.partial(per_device, sizes),
        mesh=mesh,
        in_specs=placed,
        out_specs=(
            P(None, AXES),
            P(None, None, AXES),
            P(),
            P(None, AXES),
            P(None, AXES),
        ),
        check_vma=False,
    )
```

time: 43.9 us -> 39.9 us (0.909)
  Pallas kernels: 41.3 us -> 37.3 us
    pallas_call x1, Pallas kernels: 39.4 us -> 36.5 us  [per_device(): pl.pallas_call(functools.partial(kernel, sizes, direct), out_shape=(pltpu...]
    pallas_call x1, Pallas kernels: 1.84 us -> 0.8 us  [per_device(): pl.pallas_call(write_out, out_shape=tuple((jax.ShapeDtypeStruct(r.shape,...]
where the time goes in v1:
time: 39.9 us; the launch traced here: 39.7 us
  Pallas kernels  37.3 us (93%)
  between operations  2.41 us (6%)
    pallas_call x1, Pallas kernels, per_device(): pl.pallas_call(functools.partial(kernel, sizes, direct), out_shape=(pltpu...  36.5 us
    pallas_call x1, Pallas kernels, per_device(): pl.pallas_call(write_out, out_shape=tuple((jax.ShapeDtypeStruct(r.shape,...  0.8 us

profile of v1, /device:TPU:0, one launch (start us, length us, event | category | flops | bytes accessed | tf_op | source)
XLA Modules:
  0.0 39.7 jit_solution(9041765550251424085)
XLA Ops:
  0.6 36.5 %brick.1 = (f32[64,128]{1,0:T(8,128)S(1)}, bf16[3,512,128]{2,1,0:T(8,128)(2,1)S(1)}, f32[1,1]{1,0:T(1,128)}, f32[3,2048]{1,0:T(4,128)S(1)}, f32[3,2048]{1,0:T(4,128)S(1)}) custom-call(f32[64,64,128]{2,1,0:T(8,128)} %ops_hbm.1, f32[64,128]{1,0:T(8,128)} %load_hbm.1, f32[3,512,128]{2,1,0:T(8,128)} %trial_hbm.1, bf16[3,512,256]{2,1,0:T(8,128)(2,1)} %constant.6.grad_hbm, ...), custom_call_target="tpu_custom_call" | custom-call | tf_op jit(solution)/shard_map/brick/pallas_call | solution.py:649
  37.2 0.8 %write_out.1 = (f32[64,128]{1,0:T(8,128)}, bf16[3,512,128]{2,1,0:T(8,128)(2,1)}, f32[3,2048]{1,0:T(4,128)}, f32[3,2048]{1,0:T(4,128)}) custom-call(f32[64,128]{1,0:T(8,128)S(1)} %get-tuple-element.14.refs_0_, bf16[3,512,128]{2,1,0:T(8,128)(2,1)S(1)} %get-tuple-element.15.refs_1_, f32[3,2048]{1,0:T(4,128)S(1)} %get-tuple-element.16.refs_2_, ...), custom_call_target="tpu_custom_call" | custom-call | tf_op jit(solution)/shard_map/write_out/pallas_call | solution.py:698

commit v2 on v1

--- a/solution.py
+++ b/solution.py
@@ -24,7 +24,8 @@
 COUNTS = (EX, EY, EZ)
 STEPS = (EY * EZ, EZ, 1)
 MESH = pl.DeviceIdType.MESH
-FINISH = 4
+FINISH = 3
+UNROLL = 4
 BRICK_VMEM = 24 * 1024 * 1024
 OUT_VMEM = 4 * 1024 * 1024
 
@@ -173,56 +174,6 @@
     red_send,
     red_recv,
 ):
-    me = [lax.axis_index(axis) for axis in AXES]
-    line = sizes[0]
-    groups = pay_ref.shape[1]
-
-    def edge(d, step):
-        return me[d] < sizes[d] - 1 if step > 0 else me[d] > 0
-
-    def exists(way):
-        tests = [edge(d, way[d]) for d in range(3) if way[d] != 0]
-        return functools.reduce(jnp.logical_and, tests)
-
-    present = {way: exists(way) for way in DIRS}
-
-    def beside(way):
-        return {AXES[d]: me[d] + way[d] for d in range(3) if way[d] != 0}
-
-    def along(offset):
-        there = me[0]
-        for bit in bit_moves(line):
-            if offset & bit:
-                there = there + bit * (1 - 2 * lax.rem(me[0] // bit, 2))
-        return {AXES[0]: there}
-
-    def shifted(offset):
-        return {
-            AXES[d]: lax.rem(me[d] + offset[d], sizes[d]) for d in range(3) if offset[d] != 0
-        }
-
-    spans = [range(size) for size in sizes]
-    if direct:
-        teams = [[(i, j, k) for i in spans[0] for j in spans[1] for k in spans[2]]]
-        seats = [(me[0] * sizes[1] + me[1]) * sizes[2] + me[2]]
-    else:
-        teams = [[(0, j, k) for j in spans[1] for k in spans[2]], [(i, 0, 0) for i in spans[0]]]
-        seats = [me[1] * sizes[2] + me[2], me[0]]
-    bases = [sum(len(team) for team in teams[:t]) for t in range(len(teams))]
-
-    barrier = pltpu.get_barrier_semaphore()
-    for way in DIRS:
-
-        @pl.when(present[way])
-        def _():
-            pl.semaphore_signal(barrier, inc=1, device_id=beside(way), device_id_type=MESH)
-
-    partners = [along(offset) for offset in range(1, line)]
-    if not direct:
-        partners += [shifted(offset) for team in teams for offset in team[1:]]
-    for partner in partners:
-        pl.semaphore_signal(barrier, inc=1, device_id=partner, device_id_type=MESH)
-
     pairs = [
         (ops_hbm, ops),
         (load_hbm, load),
@@ -237,8 +188,61 @@
     loads = [
         pltpu.make_async_copy(src, dst, local_sem.at[i]) for i, (src, dst) in enumerate(pairs)
     ]
-    for i in (1, 0, 2, 3, 4, 5, 6, 7, 8):
+    for i in (1, 0):
         loads[i].start()
+
+    me = [lax.axis_index(axis) for axis in AXES]
+    line = sizes[0]
+    groups = pay_ref.shape[1]
+
+    def edge(d, step):
+        return me[d] < sizes[d] - 1 if step > 0 else me[d] > 0
+
+    def exists(way):
+        tests = [edge(d, way[d]) for d in range(3) if way[d] != 0]
+        return functools.reduce(jnp.logical_and, tests)
+
+    present = {way: exists(way) for way in DIRS}
+
+    def beside(way):
+        return {AXES[d]: me[d] + way[d] for d in range(3) if way[d] != 0}
+
+    def along(offset):
+        there = me[0]
+        for bit in bit_moves(line):
+            if offset & bit:
+                there = there + bit * (1 - 2 * lax.rem(me[0] // bit, 2))
+        return {AXES[0]: there}
+
+    def shifted(offset):
+        return {
+            AXES[d]: lax.rem(me[d] + offset[d], sizes[d]) for d in range(3) if offset[d] != 0
+        }
+
+    spans = [range(size) for size in sizes]
+    if direct:
+        teams = [[(i, j, k) for i in spans[0] for j in spans[1] for k in spans[2]]]
+        seats = [(me[0] * sizes[1] + me[1]) * sizes[2] + me[2]]
+    else:
+        teams = [[(0, j, k) for j in spans[1] for k in spans[2]], [(i, 0, 0) for i in spans[0]]]
+        seats = [me[1] * sizes[2] + me[2], me[0]]
+    bases = [sum(len(team) for team in teams[:t]) for t in range(len(teams))]
+
+    barrier = pltpu.get_barrier_semaphore()
+    for way in DIRS:
+
+        @pl.when(present[way])
+        def _():
+            pl.semaphore_signal(barrier, inc=1, device_id=beside(way), device_id_type=MESH)
+
+    partners = [along(offset) for offset in range(1, line)]
+    if not direct:
+        partners += [shifted(offset) for team in teams for offset in team[1:]]
+    for partner in partners:
+        pl.semaphore_signal(barrier, inc=1, device_id=partner, device_id_type=MESH)
+
+    for copy in loads[2:7]:
+        copy.start()
 
     for way in DIRS:
 
@@ -461,6 +465,8 @@
     order = range(line - 1, 0, -1)
     for offset in order:
         pay_copy(offset).start()
+    for copy in loads[7:]:
+        copy.start()
     close_faces(0, (res, wgt))
 
     center = 0.5 * (upper_bound + lower_bound)
@@ -550,7 +556,7 @@
                     )
             return carry
 
-        lax.fori_loop(first, end, one_tile, 0)
+        lax.fori_loop(first, end, one_tile, 0, unroll=UNROLL)
 
     def finish_faces():
         drain_faces(last - 1)
@@ -596,18 +602,23 @@
             flow_ref[d : d + 1, g * LANES : (g + 1) * LANES] = flow[g : g + 1]
             moved_ref[d : d + 1, g * LANES : (g + 1) * LANES] = moved[g : g + 1]
 
-    power_ref[0, 0] = jnp.sum(close_sums(1, len(teams) - 1)) * (
-        1.0 / (float(NODES * LANES) * sizes[0] * sizes[1] * sizes[2])
+    drain_sums(1)
+    total = jnp.sum(close_sums(1, len(teams) - 1), axis=1, keepdims=True)
+    power_ref[...] = jnp.broadcast_to(
+        total * (1.0 / (float(NODES * LANES) * sizes[0] * sizes[1] * sizes[2])), (8, LANES)
     )
-    drain_sums(1)
 
 
 def write_out(*refs):
-    count = (len(refs) - 1) // 2
-    sources, targets, given = refs[:count], refs[count : 2 * count], refs[2 * count]
-    outward = [pltpu.make_async_copy(sources[i], targets[i], given.at[i]) for i in range(count)]
-    for copy in outward:
+    count = (len(refs) - 2) // 2
+    sources, targets = refs[:count], refs[count : 2 * count]
+    held, given = refs[2 * count :]
+    outward = [pltpu.make_async_copy(sources[i], targets[i], given.at[i]) for i in range(1, count)]
+    outward.append(pltpu.make_async_copy(held, targets[0], given.at[0]))
+    for copy in outward[:-1]:
         copy.start()
+    held[0, 0] = sources[0][0, 0]
+    outward[-1].start()
     for copy in outward:
         copy.wait()
 
@@ -651,12 +662,12 @@
         out_shape=(
             pltpu.VMEM((NODES, LANES), f32),
             pltpu.VMEM((3, FINE, LANES), bf16),
-            jax.ShapeDtypeStruct((1, 1), f32),
+            pltpu.VMEM((8, LANES), f32),
             pltpu.VMEM((3, count), f32),
             pltpu.VMEM((3, count), f32),
         ),
         in_specs=[hbm] * 9,
-        out_specs=(vmem, vmem, pl.BlockSpec(memory_space=pltpu.SMEM), vmem, vmem),
+        out_specs=(vmem,) * 5,
         scratch_shapes=[
             pltpu.VMEM((NODES, NODES, LANES), f32),
             pltpu.VMEM((NODES, LANES), f32),
@@ -694,17 +705,18 @@
         ),
         name="brick",
     )(*(pltpu.with_memory_space_constraint(operand, pltpu.HBM) for operand in operands))
-    results = (solution, velocity, flows, moved)
-    solution, velocity, flows, moved = pl.pallas_call(
+    results = (power, solution, velocity, flows, moved)
+    shapes = ((1, 1),) + tuple(r.shape for r in results[1:])
+    power, solution, velocity, flows, moved = pl.pallas_call(
         write_out,
-        out_shape=tuple(jax.ShapeDtypeStruct(r.shape, r.dtype) for r in results),
-        in_specs=[pl.BlockSpec(memory_space=pl.ANY)] * 4,
-        out_specs=(hbm,) * 4,
-        scratch_shapes=[dma((4,))],
+        out_shape=tuple(jax.ShapeDtypeStruct(z, r.dtype) for z, r in zip(shapes, results)),
+        in_specs=[vmem] + [pl.BlockSpec(memory_space=pl.ANY)] * 4,
+        out_specs=(hbm,) * 5,
+        scratch_shapes=[pltpu.SMEM((1, 1), f32), dma((5,))],
         compiler_params=pltpu.CompilerParams(vmem_limit_bytes=OUT_VMEM),
         name="write_out",
     )(*results)
-    return (solution, velocity, power[0, 0], flows, moved)
+    return (solution, velocity, power.reshape(()), flows, moved)
 
 
 def solution(mesh):

time: 39.9 us -> 34.8 us (0.87)
  Pallas kernels: 37.3 us -> 34 us
  between operations: 2.41 us -> 0.64 us
    pallas_call x1, Pallas kernels: 36.5 us -> 33.2 us  [per_device(): pl.pallas_call(functools.partial(kernel, sizes, direct), out_shape=(pltpu...]
where the time goes in v2:
time: 34.8 us; the launch traced here: 34.7 us
  Pallas kernels  34 us (98%)
  between operations  0.64 us (2%)
    pallas_call x1, Pallas kernels, per_device(): pl.pallas_call(functools.partial(kernel, sizes, direct), out_shape=(pltpu...  33.2 us
    pallas_call x1, Pallas kernels, per_device(): pl.pallas_call(write_out, out_shape=tuple((jax.ShapeDtypeStruct(z, r.dtyp...  0.82 us

profile of v2, /device:TPU:0, one launch (start us, length us, event | category | flops | bytes accessed | tf_op | source)
XLA Modules:
  0.0 34.7 jit_solution(13133503274992475749)
XLA Ops:
  0.6 33.2 %brick.1 = (f32[64,128]{1,0:T(8,128)S(1)}, bf16[3,512,128]{2,1,0:T(8,128)(2,1)S(1)}, f32[8,128]{1,0:T(8,128)S(1)}, f32[3,2048]{1,0:T(4,128)S(1)}, f32[3,2048]{1,0:T(4,128)S(1)}) custom-call(f32[64,64,128]{2,1,0:T(8,128)} %ops_hbm.1, f32[64,128]{1,0:T(8,128)} %load_hbm.1, f32[3,512,128]{2,1,0:T(8,128)} %trial_hbm.1, bf16[3,512,256]{2,1,0:T(8,128)(2,1)} %constant.6.grad_hbm, ...), custom_call_target="tpu_custom_call" | custom-call | tf_op jit(solution)/shard_map/brick/pallas_call | solution.py:660
  33.9 0.8 %write_out.1 = (f32[1,1]{1,0:T(1,128)}, f32[64,128]{1,0:T(8,128)}, bf16[3,512,128]{2,1,0:T(8,128)(2,1)}, f32[3,2048]{1,0:T(4,128)}, f32[3,2048]{1,0:T(4,128)}) custom-call(f32[8,128]{1,0:T(8,128)S(1)} %get-tuple-element.15.refs_0_, f32[64,128]{1,0:T(8,128)S(1)} %get-tuple-element.16.refs_1_, bf16[3,512,128]{2,1,0:T(8,128)(2,1)S(1)} %get-tuple-element.17.refs_2_, ...), custom_call_target="tpu_custom_call" | custom-call | tf_op jit(solution)/shard_map/write_out/pallas_call | solution.py:710

commit v3 on v2

--- a/solution.py
+++ b/solution.py
@@ -26,6 +26,8 @@
 MESH = pl.DeviceIdType.MESH
 FINISH = 3
 UNROLL = 4
+PAY_SWEEP = 1
+SPLIT = 8
 BRICK_VMEM = 24 * 1024 * 1024
 OUT_VMEM = 4 * 1024 * 1024
 
@@ -157,6 +159,7 @@
     img,
     work,
     wide,
+    diag,
     face_out,
     face_in,
     pay_in,
@@ -188,8 +191,16 @@
     loads = [
         pltpu.make_async_copy(src, dst, local_sem.at[i]) for i, (src, dst) in enumerate(pairs)
     ]
-    for i in (1, 0):
-        loads[i].start()
+    corners = [
+        pltpu.make_async_copy(
+            ops_hbm.at[pl.ds(n, 8), pl.ds(n, 8)], diag.at[n // 8], local_sem.at[9]
+        )
+        for n in range(0, NODES, 8)
+    ]
+    loads[1].start()
+    for copy in corners:
+        copy.start()
+    loads[0].start()
 
     me = [lax.axis_index(axis) for axis in AXES]
     line = sizes[0]
@@ -229,11 +240,12 @@
     bases = [sum(len(team) for team in teams[:t]) for t in range(len(teams))]
 
     barrier = pltpu.get_barrier_semaphore()
+    held = [
+        {w: jnp.clip(me[d] + w, 0, sizes[d] - 1) for w in (-1, 0, 1)} for d in range(3)
+    ]
     for way in DIRS:
-
-        @pl.when(present[way])
-        def _():
-            pl.semaphore_signal(barrier, inc=1, device_id=beside(way), device_id_type=MESH)
+        near = {AXES[d]: held[d][way[d]] for d in range(3) if way[d] != 0}
+        pl.semaphore_signal(barrier, inc=1, device_id=near, device_id_type=MESH)
 
     partners = [along(offset) for offset in range(1, line)]
     if not direct:
@@ -263,8 +275,8 @@
         return pltpu.make_async_remote_copy(
             src_ref=face_out.at[x, slot_of(way), pl.ds(0, rows)],
             dst_ref=face_in.at[x, there, pl.ds(0, rows)],
-            send_sem=face_send.at[x, slot_of(way)],
-            recv_sem=face_recv.at[x, there],
+            send_sem=face_send.at[x % 2, slot_of(way)],
+            recv_sem=face_recv.at[x % 2, there],
             device_id=beside(way),
             device_id_type=MESH,
         )
@@ -329,7 +341,7 @@
             at += size
 
     def close_faces(x, parts):
-        for way in DIRS:
+        for way in DIRS[::-1]:
 
             @pl.when(present[way])
             def _():
@@ -386,13 +398,16 @@
                 total = total + ops[8 * i + j] * rows[j : j + 1, :]
             return total
 
-        img[...] = lax.fori_loop(0, NODES // 8, block, jnp.zeros((NODES, LANES), jnp.float32))
+        img[...] = lax.fori_loop(0, NODES // 8, block, jnp.zeros((NODES, LANES), jnp.float32), unroll=SPLIT)
+
+    def settle(view, sem):
+        pltpu.make_async_copy(view, view, sem).wait()
 
     def pay_copy(offset):
         return pltpu.make_async_remote_copy(
             src_ref=pay_ref,
             dst_ref=pay_in.at[offset - 1],
-            send_sem=pay_send.at[offset - 1],
+            send_sem=pay_send.at[0],
             recv_sem=pay_recv.at[offset - 1],
             device_id=along(offset),
             device_id_type=MESH,
@@ -402,8 +417,8 @@
         return pltpu.make_async_remote_copy(
             src_ref=back_out.at[offset],
             dst_ref=back_in.at[offset - 1],
-            send_sem=back_send.at[offset - 1],
-            recv_sem=back_recv.at[offset - 1],
+            send_sem=back_send.at[0],
+            recv_sem=back_recv.at[0],
             device_id=along(offset),
             device_id_type=MESH,
         )
@@ -412,11 +427,14 @@
         return pltpu.make_async_remote_copy(
             src_ref=red_out.at[kind, t, pl.ds(0, 1)],
             dst_ref=red_in.at[kind, bases[t] + seats[t], pl.ds(0, 1)],
-            send_sem=red_send.at[kind, bases[t] + offset],
-            recv_sem=red_recv.at[kind, bases[t] + offset],
+            send_sem=red_send.at[kind, t],
+            recv_sem=red_recv.at[kind, t],
             device_id=shifted(teams[t][offset]),
             device_id_type=MESH,
         )
+
+    def others(kind, t):
+        return red_in.at[kind, pl.ds(bases[t], len(teams[t]) - 1), pl.ds(0, 1)]
 
     def open_sums(kind, t, value):
         red_out[kind, t, 0:1] = value
@@ -425,8 +443,7 @@
         red_in[kind, bases[t] + seats[t], 0:1] = value
 
     def close_sums(kind, t):
-        for offset in range(1, len(teams[t])):
-            red_copy(kind, t, offset).wait_recv()
+        settle(others(kind, t), red_recv.at[kind, t])
         values = [red_in[kind, bases[t] + i, 0:1] for i in range(len(teams[t]))]
         join = jnp.add if kind else jnp.maximum
         while len(values) > 1:
@@ -437,16 +454,18 @@
         return values[0]
 
     def drain_sums(kind):
-        for t, team in enumerate(teams):
-            for offset in range(1, len(team)):
-                red_copy(kind, t, offset).wait_send()
+        for t in range(len(teams)):
+            settle(others(kind, t), red_send.at[kind, t])
 
     loads[1].wait()
-    loads[0].wait()
+    settle(ops.at[pl.ds(0, 8)], local_sem.at[9])
     res[...] = load[...]
     for n in range(NODES):
-        wgt[n : n + 1, :] = ops[n, n : n + 1, :]
+        wgt[n : n + 1, :] = diag[n // 8, n % 8, n % 8 : n % 8 + 1, :]
     fill_faces(0, (res, wgt), DIRS)
+    pl.semaphore_wait(barrier, len(partners) + len(DIRS))
+
+    start_faces(0, DIRS)
     for copy in loads[2:7]:
         copy.wait()
     pay_ref[3] = (host[...] * LANES + index[...]).astype(jnp.float32)
@@ -455,20 +474,12 @@
             lanes = slice(g * LANES, (g + 1) * LANES)
             pay_ref[d, g : g + 1, :] = coords[d : d + 1, lanes]
             old_ref[d, g : g + 1, :] = old[d : d + 1, lanes]
-
-    near = [sum(edge(d, step).astype(jnp.int32) for step in (-1, 1)) for d in range(3)]
-    pl.semaphore_wait(
-        barrier, len(partners) + (1 + near[0]) * (1 + near[1]) * (1 + near[2]) - 1
-    )
-
-    start_faces(0, DIRS)
     order = range(line - 1, 0, -1)
-    for offset in order:
-        pay_copy(offset).start()
     for copy in loads[7:]:
         copy.start()
     close_faces(0, (res, wgt))
 
+    loads[0].wait()
     center = 0.5 * (upper_bound + lower_bound)
     radius = 0.5 * (upper_bound - lower_bound)
     sigma = center / radius
@@ -478,12 +489,14 @@
     for sweep in range(SWEEPS - 1):
         apply_operator()
         open_faces(sweep + 1, (img,))
+        if sweep == PAY_SWEEP:
+            for offset in order:
+                pay_copy(offset).start()
         drain_faces(sweep)
         if sweep + 2 == SWEEPS:
             for copy in loads[7:]:
                 copy.wait()
-            for offset in order:
-                pay_copy(offset).wait_send()
+            settle(pay_in, pay_send.at[0])
         close_faces(sweep + 1, (img,))
         left = res[...] - img[...]
         res[...] = left
@@ -589,10 +602,8 @@
     stride = courant / (jnp.max(most, axis=1, keepdims=True) + 1e-06)
     stride = jnp.broadcast_to(stride, (groups, LANES))
     drain_sums(0)
-    for offset in order:
-        back_copy(offset).wait_send()
-    for offset in order:
-        back_copy(offset).wait_recv()
+    settle(back_in, back_send.at[0])
+    settle(back_in, back_recv.at[0])
     for d in range(3):
         flow = back_out[0, d]
         for offset in range(1, line):
@@ -683,6 +694,7 @@
             *small,
             pltpu.VMEM((4, 40, LANES), f32),
             pltpu.VMEM((3 * NODES, 8 * LANES), bf16),
+            pltpu.VMEM((NODES // 8, 8, 8, LANES), f32),
             pltpu.VMEM((SWEEPS + 1, 27, 2 * FACE, LANES), f32),
             pltpu.VMEM((SWEEPS + 1, 27, 2 * FACE, LANES), f32),
             pltpu.VMEM((line - 1, 4, groups, LANES), f32),
@@ -690,15 +702,15 @@
             pltpu.VMEM((line - 1, 3, groups, LANES), f32),
             pltpu.VMEM((2, 2, 8, LANES), f32),
             pltpu.VMEM((2, seats, 8, LANES), f32),
-            dma((9,)),
-            dma((SWEEPS + 1, 27)),
-            dma((SWEEPS + 1, 27)),
+            dma((10,)),
+            dma((2, 27)),
+            dma((2, 27)),
+            dma((1,)),
             dma((line - 1,)),
-            dma((line - 1,)),
-            dma((line - 1,)),
-            dma((line - 1,)),
-            dma((2, seats)),
-            dma((2, seats)),
+            dma((1,)),
+            dma((1,)),
+            dma((2, 1 if direct else 2)),
+            dma((2, 1 if direct else 2)),
         ],
         compiler_params=pltpu.CompilerParams(
             collective_id=0, has_side_effects=True, vmem_limit_bytes=BRICK_VMEM

time: 34.8 us -> 31.6 us (0.908)
  Pallas kernels: 34 us -> 30.9 us
    pallas_call x1, Pallas kernels: 33.2 us -> 30 us  [per_device(): pl.pallas_call(functools.partial(kernel, sizes, direct), out_shape=(pltpu...]
where the time goes in v3:
time: 31.6 us; the launch traced here: 31.5 us
  Pallas kernels  30.9 us (98%)
  between operations  0.64 us (2%)
    pallas_call x1, Pallas kernels, per_device(): pl.pallas_call(functools.partial(kernel, sizes, direct), out_shape=(pltpu...  30 us
    pallas_call x1, Pallas kernels, per_device(): pl.pallas_call(write_out, out_shape=tuple((jax.ShapeDtypeStruct(z, r.dtyp...  0.82 us

profile of v3, /device:TPU:0, one launch (start us, length us, event | category | flops | bytes accessed | tf_op | source)
XLA Modules:
  0.0 31.5 jit_solution(8688103864240107706)
XLA Ops:
  0.6 30.0 %brick.1 = (f32[64,128]{1,0:T(8,128)S(1)}, bf16[3,512,128]{2,1,0:T(8,128)(2,1)S(1)}, f32[8,128]{1,0:T(8,128)S(1)}, f32[3,2048]{1,0:T(4,128)S(1)}, f32[3,2048]{1,0:T(4,128)S(1)}) custom-call(f32[64,64,128]{2,1,0:T(8,128)} %ops_hbm.1, f32[64,128]{1,0:T(8,128)} %load_hbm.1, f32[3,512,128]{2,1,0:T(8,128)} %trial_hbm.1, bf16[3,512,256]{2,1,0:T(8,128)(2,1)} %constant.6.grad_hbm, ...), custom_call_target="tpu_custom_call" | custom-call | tf_op jit(solution)/shard_map/brick/pallas_call | solution.py:671
  30.7 0.8 %write_out.1 = (f32[1,1]{1,0:T(1,128)}, f32[64,128]{1,0:T(8,128)}, bf16[3,512,128]{2,1,0:T(8,128)(2,1)}, f32[3,2048]{1,0:T(4,128)}, f32[3,2048]{1,0:T(4,128)}) custom-call(f32[8,128]{1,0:T(8,128)S(1)} %get-tuple-element.15.refs_0_, f32[64,128]{1,0:T(8,128)S(1)} %get-tuple-element.16.refs_1_, bf16[3,512,128]{2,1,0:T(8,128)(2,1)S(1)} %get-tuple-element.17.refs_2_, ...), custom_call_target="tpu_custom_call" | custom-call | tf_op jit(solution)/shard_map/write_out/pallas_call | solution.py:722

commit v4 on v3

--- a/solution.py
+++ b/solution.py
@@ -1,4 +1,6 @@
 import functools
+import itertools
+import math
 
 import jax
 import jax.numpy as jnp
@@ -160,6 +162,7 @@
     work,
     wide,
     diag,
+    bulk,
     face_out,
     face_in,
     pay_in,
@@ -275,8 +278,8 @@
         return pltpu.make_async_remote_copy(
             src_ref=face_out.at[x, slot_of(way), pl.ds(0, rows)],
             dst_ref=face_in.at[x, there, pl.ds(0, rows)],
-            send_sem=face_send.at[x % 2, slot_of(way)],
-            recv_sem=face_recv.at[x % 2, there],
+            send_sem=face_send.at[x % 2],
+            recv_sem=face_recv.at[x % 2],
             device_id=beside(way),
             device_id_type=MESH,
         )
@@ -296,12 +299,30 @@
             def _():
                 face_copy(x, way).start()
 
+    def settle(view, sem):
+        pltpu.make_async_copy(view, view, sem).wait()
+
+    between = [jnp.logical_and(edge(d, -1), edge(d, 1)) for d in range(3)]
+
+    def settle_faces(x, sem):
+        for near in itertools.product(*[(min(size - 1, 1), 2)[: min(size - 1, 2)] for size in sizes]):
+            rows = sum(
+                length_of(way) * math.prod(near[d] for d in range(3) if way[d])
+                for way in itertools.product((0, 1), repeat=3)
+                if any(way)
+            )
+            tests = [
+                between[d] if near[d] == 2 else jnp.logical_not(between[d])
+                for d in range(3)
+                if sizes[d] > 2
+            ]
+
+            @pl.when(functools.reduce(jnp.logical_and, tests))
+            def _():
+                settle(bulk.at[pl.ds(0, parts_of(x) * rows)], sem)
+
     def drain_faces(x):
-        for way in DIRS:
-
-            @pl.when(present[way])
-            def _():
-                face_copy(x, way).wait_send()
+        settle_faces(x, face_send.at[x % 2])
 
     def open_faces(x, parts):
         for group in (DIRS[:8], DIRS[8:20], DIRS[20:]):
@@ -341,11 +362,7 @@
             at += size
 
     def close_faces(x, parts):
-        for way in DIRS[::-1]:
-
-            @pl.when(present[way])
-            def _():
-                face_copy(x, tuple(-w for w in way)).wait_recv()
+        settle_faces(x, face_recv.at[x % 2])
 
         ends = (-1, 1)
         for p, ref in enumerate(parts):
@@ -399,9 +416,6 @@
             return total
 
         img[...] = lax.fori_loop(0, NODES // 8, block, jnp.zeros((NODES, LANES), jnp.float32), unroll=SPLIT)
-
-    def settle(view, sem):
-        pltpu.make_async_copy(view, view, sem).wait()
 
     def pay_copy(offset):
         return pltpu.make_async_remote_copy(
@@ -695,6 +709,7 @@
             pltpu.VMEM((4, 40, LANES), f32),
             pltpu.VMEM((3 * NODES, 8 * LANES), bf16),
             pltpu.VMEM((NODES // 8, 8, 8, LANES), f32),
+            pltpu.VMEM((20 * FACE, LANES), f32),
             pltpu.VMEM((SWEEPS + 1, 27, 2 * FACE, LANES), f32),
             pltpu.VMEM((SWEEPS + 1, 27, 2 * FACE, LANES), f32),
             pltpu.VMEM((line - 1, 4, groups, LANES), f32),
@@ -703,8 +718,8 @@
             pltpu.VMEM((2, 2, 8, LANES), f32),
             pltpu.VMEM((2, seats, 8, LANES), f32),
             dma((10,)),
-            dma((2, 27)),
-            dma((2, 27)),
+            dma((2,)),
+            dma((2,)),
             dma((1,)),
             dma((line - 1,)),
             dma((1,)),

time: 31.6 us -> 30.7 us (0.972)
  Pallas kernels: 30.9 us -> 29.9 us
    pallas_call x1, Pallas kernels: 30 us -> 29.1 us  [per_device(): pl.pallas_call(functools.partial(kernel, sizes, direct), out_shape=(pltpu...]
where the time goes in v4:
time: 30.7 us; the launch traced here: 30.5 us
  Pallas kernels  29.9 us (97%)
  between operations  0.64 us (2%)
    pallas_call x1, Pallas kernels, per_device(): pl.pallas_call(functools.partial(kernel, sizes, direct), out_shape=(pltpu...  29.1 us
    pallas_call x1, Pallas kernels, per_device(): pl.pallas_call(write_out, out_shape=tuple((jax.ShapeDtypeStruct(z, r.dtyp...  0.82 us

profile of v4, /device:TPU:0, one launch (start us, length us, event | category | flops | bytes accessed | tf_op | source)
XLA Modules:
  0.0 30.5 jit_solution(16609937110281722095)
XLA Ops:
  0.6 29.1 %brick.1 = (f32[64,128]{1,0:T(8,128)S(1)}, bf16[3,512,128]{2,1,0:T(8,128)(2,1)S(1)}, f32[8,128]{1,0:T(8,128)S(1)}, f32[3,2048]{1,0:T(4,128)S(1)}, f32[3,2048]{1,0:T(4,128)S(1)}) custom-call(f32[64,64,128]{2,1,0:T(8,128)} %ops_hbm.1, f32[64,128]{1,0:T(8,128)} %load_hbm.1, f32[3,512,128]{2,1,0:T(8,128)} %trial_hbm.1, bf16[3,512,256]{2,1,0:T(8,128)(2,1)} %constant.6.grad_hbm, ...), custom_call_target="tpu_custom_call" | custom-call | tf_op jit(solution)/shard_map/brick/pallas_call | solution.py:685
  29.7 0.8 %write_out.1 = (f32[1,1]{1,0:T(1,128)}, f32[64,128]{1,0:T(8,128)}, bf16[3,512,128]{2,1,0:T(8,128)(2,1)}, f32[3,2048]{1,0:T(4,128)}, f32[3,2048]{1,0:T(4,128)}) custom-call(f32[8,128]{1,0:T(8,128)S(1)} %get-tuple-element.15.refs_0_, f32[64,128]{1,0:T(8,128)S(1)} %get-tuple-element.16.refs_1_, bf16[3,512,128]{2,1,0:T(8,128)(2,1)S(1)} %get-tuple-element.17.refs_2_, ...), custom_call_target="tpu_custom_call" | custom-call | tf_op jit(solution)/shard_map/write_out/pallas_call | solution.py:737

commit v5 on v4

--- a/solution.py
+++ b/solution.py
@@ -28,7 +28,6 @@
 MESH = pl.DeviceIdType.MESH
 FINISH = 3
 UNROLL = 4
-PAY_SWEEP = 1
 SPLIT = 8
 BRICK_VMEM = 24 * 1024 * 1024
 OUT_VMEM = 4 * 1024 * 1024
@@ -83,14 +82,15 @@
     return table
 
 
-DIRS = [
-    (i, j, k)
-    for size in (3, 2, 1)
-    for i in (-1, 0, 1)
-    for j in (-1, 0, 1)
-    for k in (-1, 0, 1)
-    if abs(i) + abs(j) + abs(k) == size
-]
+def rank(way):
+    size = sum(abs(w) for w in way)
+    return -1 if size == 2 and way[1] == 0 else 3 - size
+
+
+DIRS = sorted(
+    ((i, j, k) for i in (-1, 0, 1) for j in (-1, 0, 1) for k in (-1, 0, 1) if i or j or k),
+    key=rank,
+)
 
 
 def slot_of(way):
@@ -221,17 +221,20 @@
     def beside(way):
         return {AXES[d]: me[d] + way[d] for d in range(3) if way[d] != 0}
 
+    def moved_by(d, offset):
+        there = me[d]
+        for bit in bit_moves(sizes[d]):
+            if offset & bit:
+                there = there + bit * (1 - 2 * lax.rem(me[d] // bit, 2))
+        return there
+
+    moves = [[moved_by(d, offset) for offset in range(sizes[d])] for d in range(3)]
+
     def along(offset):
-        there = me[0]
-        for bit in bit_moves(line):
-            if offset & bit:
-                there = there + bit * (1 - 2 * lax.rem(me[0] // bit, 2))
-        return {AXES[0]: there}
+        return {AXES[0]: moves[0][offset]}
 
     def shifted(offset):
-        return {
-            AXES[d]: lax.rem(me[d] + offset[d], sizes[d]) for d in range(3) if offset[d] != 0
-        }
+        return {AXES[d]: moves[d][offset[d]] for d in range(3) if offset[d] != 0}
 
     spans = [range(size) for size in sizes]
     if direct:
@@ -259,18 +262,20 @@
     for copy in loads[2:7]:
         copy.start()
 
-    for way in DIRS:
-
-        @pl.when(jnp.logical_not(present[way]))
-        def _():
-            for x in range(SWEEPS + 1):
-                face_in[x, slot_of(way)] = jnp.zeros((2 * FACE, LANES), jnp.float32)
-
     lane = lax.broadcasted_iota(jnp.int32, (40, LANES), 1)
     place = [lane // (EY * EZ), lane // EZ % EY, lane % EZ]
 
     def parts_of(x):
         return 2 if x == 0 else 1
+
+    def clear_faces(rounds):
+        for way in DIRS:
+
+            @pl.when(jnp.logical_not(present[way]))
+            def _():
+                for x in rounds:
+                    rows = -(-parts_of(x) * length_of(way) // 8) * 8
+                    face_in[x, slot_of(way), 0:rows] = jnp.zeros((rows, LANES), jnp.float32)
 
     def face_copy(x, way):
         rows = parts_of(x) * length_of(way)
@@ -325,7 +330,7 @@
         settle_faces(x, face_send.at[x % 2])
 
     def open_faces(x, parts):
-        for group in (DIRS[:8], DIRS[8:20], DIRS[20:]):
+        for group in (DIRS[:12], DIRS[12:20], DIRS[20:]):
             fill_faces(x, parts, group)
             start_faces(x, group)
 
@@ -480,6 +485,7 @@
     pl.semaphore_wait(barrier, len(partners) + len(DIRS))
 
     start_faces(0, DIRS)
+    clear_faces(range(SWEEPS + 1))
     for copy in loads[2:7]:
         copy.wait()
     pay_ref[3] = (host[...] * LANES + index[...]).astype(jnp.float32)
@@ -503,8 +509,8 @@
     for sweep in range(SWEEPS - 1):
         apply_operator()
         open_faces(sweep + 1, (img,))
-        if sweep == PAY_SWEEP:
-            for offset in order:
+        for turn, offset in enumerate(order):
+            if sweep == min(turn, SWEEPS - 2):
                 pay_copy(offset).start()
         drain_faces(sweep)
         if sweep + 2 == SWEEPS:

time: 30.7 us -> 30.5 us (level)
  no operation moved by 1% of the time
where the time goes in v5:
time: 30.5 us; the launch traced here: 30.3 us
  Pallas kernels  29.7 us (97%)
  between operations  0.64 us (2%)
    pallas_call x1, Pallas kernels, per_device(): pl.pallas_call(functools.partial(kernel, sizes, direct), out_shape=(pltpu...  28.9 us
    pallas_call x1, Pallas kernels, per_device(): pl.pallas_call(write_out, out_shape=tuple((jax.ShapeDtypeStruct(z, r.dtyp...  0.82 us

profile of v5, /device:TPU:0, one launch (start us, length us, event | category | flops | bytes accessed | tf_op | source)
XLA Modules:
  0.0 30.3 jit_solution(9574184032238064813)
XLA Ops:
  0.6 28.9 %brick.1 = (f32[64,128]{1,0:T(8,128)S(1)}, bf16[3,512,128]{2,1,0:T(8,128)(2,1)S(1)}, f32[8,128]{1,0:T(8,128)S(1)}, f32[3,2048]{1,0:T(4,128)S(1)}, f32[3,2048]{1,0:T(4,128)S(1)}) custom-call(f32[64,64,128]{2,1,0:T(8,128)} %ops_hbm.1, f32[64,128]{1,0:T(8,128)} %load_hbm.1, f32[3,512,128]{2,1,0:T(8,128)} %trial_hbm.1, bf16[3,512,256]{2,1,0:T(8,128)(2,1)} %constant.6.grad_hbm, ...), custom_call_target="tpu_custom_call" | custom-call | tf_op jit(solution)/shard_map/brick/pallas_call | solution.py:691
  29.5 0.8 %write_out.1 = (f32[1,1]{1,0:T(1,128)}, f32[64,128]{1,0:T(8,128)}, bf16[3,512,128]{2,1,0:T(8,128)(2,1)}, f32[3,2048]{1,0:T(4,128)}, f32[3,2048]{1,0:T(4,128)}) custom-call(f32[8,128]{1,0:T(8,128)S(1)} %get-tuple-element.15.refs_0_, f32[64,128]{1,0:T(8,128)S(1)} %get-tuple-element.16.refs_1_, bf16[3,512,128]{2,1,0:T(8,128)(2,1)S(1)} %get-tuple-element.17.refs_2_, ...), custom_call_target="tpu_custom_call" | custom-call | tf_op jit(solution)/shard_map/write_out/pallas_call | solution.py:743
